TPU v7x, 128 devices: a whole 4x4x4 slice. The times are simulated.
128 devices in a mesh: tx: 8 (over z_hi, y), ty: 16 (over x, z_lo, core).
Axes of the slice: x: 4, y: 4, z: 4 (z_hi: 2, z_lo: 2; z = z_hi * 2 + z_lo), core: 2. Of those that a mesh axis runs over, the one named last changes fastest.
Arguments:
- states: bfloat16 [2, 256, 16384], P(None, 'ty', 'tx')
- norm_gain: bfloat16 [16384], P('tx'), may hold values from 0.099609375 to 1.8984375
- w_gate: bfloat16 [16384, 26624], P('tx', 'ty'), may hold values from -0.046875 to 0.046875
- w_up: bfloat16 [16384, 26624], P('tx', 'ty'), may hold values from -0.046875 to 0.046875
- w_down: bfloat16 [26624, 16384], P('ty', 'tx'), may hold values from -0.0390625 to 0.0390625
- w_qkv: bfloat16 [16384, 3, 4096], P('tx', None, 'ty'), may hold values from -0.046875 to 0.046875
- w_class: bfloat16 [4096, 14], P('ty'), may hold values from -0.375 to 0.375
- cache_keys: bfloat16 [256, 64, 4096], P('tx', None, 'ty')
- cache_values: bfloat16 [256, 64, 4096], P('tx', None, 'ty'), may hold values from -6 to 6
- cache_lengths: int32 [256], P('tx'), may hold values from 1 to 64, as said below
- row_slots: int32 [256], replicated, may hold values from 0 to 255, each once
Outputs:
- stream_out: bfloat16 [2, 256, 16384], P(None, 'ty', 'tx')
- category_logits: float32 [2, 256, 14], replicated
Inputs may be any that keep to these rules, and one draw needn't show every extreme that they name: `cache_lengths`: some slot has exactly 64 live positions. `row_slots`: each cache slot belongs to exactly one row.
All inputs are finite; a program needn't handle non-finite values.
Results may differ from a plain program's by a relative error of at most 0.015.
The roundings to bfloat16 on the way count: a program that leaves them out, or rounds other values in their place, can miss the bound.
Values may be sent and summed in bfloat16 or wider, within the bound.
No kernel may reach another device: no remote copies, remote signals or barrier semaphores. Data moves between devices by JAX's collectives and lax.ppermute only.
A program may use at most 128 MiB of HBM per device.

v0:
```python
import jax
import jax.numpy as jnp
from jax import lax
from jax.sharding import PartitionSpec as P

D = 16384
HEAD_DIM = 128


def per_device(
    states,
    norm_gain,
    w_gate,
    w_up,
    w_down,
    w_qkv,
    w_class,
    cache_keys,
    cache_values,
    cache_lengths,
    row_slots,
):
    steps_count = states.shape[0]
    local_rows = states.shape[1]
    total_rows = row_slots.shape[0]
    owner_rows = cache_keys.shape[0]
    history = cache_keys.shape[1]
    local_width = w_qkv.shape[2]
    heads_here = local_width // HEAD_DIM
    values_f = states.astype(jnp.float32)
    squares = lax.psum(jnp.sum(values_f * values_f, axis=2), "tx")
    scale = lax.rsqrt(squares / D + 1e-05)
    normed_local = (values_f * scale[:, :, None] * norm_gain.astype(jnp.float32)).astype(
        jnp.bfloat16
    )
    normed = lax.all_gather(normed_local, "ty", axis=1, tiled=True)
    slot_rows = (
        jnp.zeros((total_rows,), jnp.int32)
        .at[row_slots]
        .set(jnp.arange(total_rows, dtype=jnp.int32))
    )
    qkv_weight = w_qkv.reshape(w_qkv.shape[0], 3 * local_width)
    outputs = []
    partials = []
    new_keys = []
    new_values = []
    for step in range(steps_count):
        normed_step = normed[step]
        gate, up = lax.psum(
            (
                jnp.dot(normed_step, w_gate, preferred_element_type=jnp.float32),
                jnp.dot(normed_step, w_up, preferred_element_type=jnp.float32),
            ),
            "tx",
        )
        hidden = (jax.nn.silu(gate) * up).astype(jnp.bfloat16)

        def down_term(start, count, source=hidden):
            return jnp.dot(source, w_down, preferred_element_type=jnp.float32)

        mixed = lax.psum_scatter(
            down_term(jnp.int32(0), local_rows * lax.axis_size("ty")),
            "ty",
            scatter_dimension=0,
            tiled=True,
        )
        stream = (values_f[step] + mixed).astype(jnp.bfloat16)
        outputs.append(stream)
        stream_all = lax.all_gather(stream, "ty", axis=0, tiled=True)
        ordered = jnp.take(stream_all, slot_rows, axis=0)
        full = lax.psum(jnp.dot(ordered, qkv_weight, preferred_element_type=jnp.float32), "tx")
        owned = lax.dynamic_slice_in_dim(full, lax.axis_index("tx") * owner_rows, owner_rows, 0)
        triple = owned.astype(jnp.bfloat16).reshape(owner_rows, 3, local_width)
        query = triple[:, 0]
        new_keys.append(triple[:, 1])
        new_values.append(triple[:, 2])
        keys = jnp.concatenate([cache_keys, jnp.stack(new_keys, axis=1)], axis=1)
        vals = jnp.concatenate([cache_values, jnp.stack(new_values, axis=1)], axis=1)
        count_keys = keys.shape[1]
        query_h = query.reshape(owner_rows, heads_here, HEAD_DIM)
        keys_h = keys.reshape(owner_rows, count_keys, heads_here, HEAD_DIM)
        vals_h = vals.reshape(owner_rows, count_keys, heads_here, HEAD_DIM)
        scores = jnp.einsum(
            "shd,slhd->shl", query_h, keys_h, preferred_element_type=jnp.float32
        ) * HEAD_DIM ** (-0.5)
        where_pos = jnp.arange(count_keys, dtype=jnp.int32)
        valid = (where_pos[None, :] < cache_lengths[:, None]) | (where_pos[None, :] >= history)
        scores = jnp.where(valid[:, None, :], scores, jnp.float32(-1e30))
        top = jnp.max(scores, axis=2, keepdims=True)
        expo = jnp.exp(scores - top)
        weights = (expo / jnp.sum(expo, axis=2, keepdims=True)).astype(jnp.bfloat16)
        attended = jnp.einsum("shl,slhd->shd", weights, vals_h, preferred_element_type=jnp.float32)
        attended = attended.reshape(owner_rows, local_width).astype(jnp.bfloat16)
        partials.append(jnp.dot(attended, w_class, preferred_element_type=jnp.float32))
    stacked = jnp.stack(partials, axis=0)
    summed = lax.psum(stacked, "ty")
    by_slot = lax.all_gather(summed, "tx", axis=1, tiled=True)
    category_logits = jnp.take(by_slot, row_slots, axis=1)
    return (jnp.stack(outputs, axis=0), category_logits)


def solution(mesh):
    return jax.shard_map(
        per_device,
        mesh=mesh,
        in_specs=(
            P(None, "ty", "tx"),
            P("tx"),
            P("tx", "ty"),
            P("tx", "ty"),
            P("ty", "tx"),
            P("tx", None, "ty"),
            P("ty", None),
            P("tx", None, "ty"),
            P("tx", None, "ty"),
            P("tx"),
            P(),
        ),
        out_specs=(P(None, "ty", "tx"), P()),
        check_vma=False,
    )
```

profile of v0, /device:TPU:0, one launch (start us, length us, event | category | flops | bytes accessed | tf_op | source)
XLA Modules:
  0.0 643.5 jit_solution(3496387815426926068)
XLA Ops:
  8.9 25.4 %psum.56 = f32[2,16]{1,0:T(2,128)S(1)} all-reduce(f32[2,16]{1,0:T(2,128)S(1)} %multiply_reduce_fusion), channel_id=1, replica_groups=mesh['tx'=8,'ty'=16] {'tx'}, use_global_device_ids=true, to_apply=%region_1.0 | all-reduce | flops 32 | bytes 256 | tf_op jit(solution)/shard_map/psum | solution.py:31
  36.0 30.8 %all-gather.4.cloned.1.call-done = bf16[2,256,2048]{2,1,0:T(8,128)(2,1)} async-done(((bf16[2,16,2048]{2,1,0:T(8,128)(2,1)}), bf16[2,256,2048]{2,1,0:T(8,128)(2,1)}) %all-gather.4.cloned.1.call-update) | async-done | bytes 2097168 | tf_op jit(solution)/shard_map/all_gather | solution.py:36
  66.9 6.7 %fusion.28 = f32[256,1664]{1,0:T(8,128)} fusion(bf16[2048,1664]{1,0:T(8,128)(2,1)} %param.16, bf16[2,256,2048]{2,1,0:T(8,128)(2,1)} %all-gather.4.cloned.1.call-done), kind=kOutput, calls=%fused_computation.42 | convolution fusion | flops 1744830464 | bytes 9568256 | tf_op jit(solution)/shard_map/dot_general | solution.py:52
  73.6 6.4 fusion.30
  80.0 3.3 fusion.29
  83.3 3.3 fusion.31
  86.6 157.6 %all-reduce.5.cloned.1.call-done = (f32[256,1664]{1,0:T(8,128)}, f32[256,1664]{1,0:T(8,128)}, f32[256,1664]{1,0:T(8,128)}, f32[256,1664]{1,0:T(8,128)}) async-done(((f32[256,1664]{1,0:T(8,128)}, f32[256,1664]{1,0:T(8,128)}, f32[256,1664]{1,0:T(8,128)}, f32[256,1664]{1,0:T(8,128)}), (f32[256,1664]{1,0:T(8,128)}, f32[256,1664]{1,0:T(8,128)}, f32[256,1664]{1,0:T(8,128)}, ...) | async-done | bytes 6815760 | tf_op jit(solution)/shard_map/psum | solution.py:49
  244.2 7.5 %fusion.33 = f32[256,2048]{1,0:T(8,128)} fusion(bf16[1664,2048]{1,0:T(8,128)(2,1)} %param.17, f32[256,1664]{1,0:T(8,128)} %get-tuple-element.13, f32[256,1664]{1,0:T(8,128)} %get-tuple-element.14), kind=kOutput, calls=%fused_computation.47 | convolution fusion | flops 1747386368 | bytes 12320768 | tf_op jit(solution)/shard_map/dot_general | solution.py:59
  253.1 7.0 %fusion.32 = f32[256,2048]{1,0:T(8,128)} fusion(bf16[1664,2048]{1,0:T(8,128)(2,1)} %param.17, f32[256,1664]{1,0:T(8,128)S(1)} %copy-done.11, f32[256,1664]{1,0:T(8,128)} %get-tuple-element.16), kind=kOutput, calls=%fused_computation.46 | convolution fusion | flops 1747386368 | bytes 12320768 | tf_op jit(solution)/shard_map/dot_general | solution.py:59
  260.3 53.0 %reduce-scatter.5.cloned.1.call-done = f32[16,2048]{1,0:T(8,128)} async-done(((f32[256,2048]{1,0:T(8,128)}), f32[16,2048]{1,0:T(8,128)}) %reduce-scatter.5.cloned.1.call-update) | async-done | bytes 131088 | tf_op jit(solution)/shard_map/reduce_scatter | solution.py:61
  313.3 64.4 %reduce-scatter.3.cloned.1.call-done = f32[16,2048]{1,0:T(8,128)} async-done(((f32[256,2048]{1,0:T(8,128)}), f32[16,2048]{1,0:T(8,128)}) %reduce-scatter.3.cloned.1.call-update) | async-done | bytes 131088 | tf_op jit(solution)/shard_map/reduce_scatter | solution.py:61
  377.7 1.7 fusion.41
  380.1 3.1 copy.28
  385.5 24.7 %all-gather.8.cloned.1.call-done = bf16[256,2048]{1,0:T(8,128)(2,1)} async-done(((bf16[16,2048]{1,0:T(8,128)(2,1)}), bf16[256,2048]{1,0:T(8,128)(2,1)}) %all-gather.8.cloned.1.call-update) | async-done | bytes 1048592 | tf_op jit(solution)/shard_map/all_gather | solution.py:69
  410.2 4.7 gather_fusion.2
  415.0 3.2 fusion.22
  418.2 26.1 %all-gather.6.cloned.1.call-done = bf16[256,2048]{1,0:T(8,128)(2,1)} async-done(((bf16[16,2048]{1,0:T(8,128)(2,1)}), bf16[256,2048]{1,0:T(8,128)(2,1)}) %all-gather.6.cloned.1.call-update) | async-done | bytes 1048592 | tf_op jit(solution)/shard_map/all_gather | solution.py:69
  444.3 4.7 gather_fusion.1
  449.0 3.2 fusion.24
  452.2 83.2 %all-reduce.6 = (bf16[256,768]{1,0:T(8,128)(2,1)S(1)}, bf16[256,768]{1,0:T(8,128)(2,1)S(1)}) all-reduce(f32[256,768]{1,0:T(8,128)} %fusion.22, f32[256,768]{1,0:T(8,128)} %fusion.24), channel_id=1, replica_groups=mesh['tx'=8,'ty'=16] {'tx'}, use_global_device_ids=true, to_apply=%region_12.14 | all-reduce | flops 393216 | bytes 2359296 | tf_op jit(solution)/shard_map/psum | solution.py:71
  537.0 1.9 fusion.10
  543.8 1.9 fusion.6
  547.2 52.9 %psum.63 = f32[2,32,14]{1,2,0:T(8,128)S(1)} all-reduce(f32[2,32,14]{1,2,0:T(8,128)S(1)} %pad_maximum_fusion.5), channel_id=1, replica_groups=mesh['tx'=8,'ty'=16] {'ty'}, use_global_device_ids=true, to_apply=%region_15.17 | all-reduce | flops 896 | bytes 7168 | tf_op jit(solution)/shard_map/psum | solution.py:96
  600.2 34.4 %all_gather.15 = f32[2,256,14]{2,0,1:T(2,128)S(1)} all-gather(f32[2,32,14]{2,0,1:T(2,128)S(1)} %copy.33), channel_id=1, replica_groups=mesh['tx'=8,'ty'=16] {'tx'}, dimensions={1}, use_global_device_ids=true | all-gather | bytes 32256 | tf_op jit(solution)/shard_map/all_gather | solution.py:97
  (85 shorter events, 17.9 us)
Async XLA Ops:
  7.2 539.8 %copy-start = (bf16[256,14]{0,1:T(8,128)(2,1)S(1)}, bf16[256,14]{0,1:T(8,128)(2,1)}, u32[]{:S(2)}) copy-start(bf16[256,14]{0,1:T(8,128)(2,1)} %param.19) | copy-start | bytes 21508
  7.2 59.7 %all-gather.4.cloned.1.call-start = ((), (), s32[]{:S(2)}) async-start(), calls=%async_computation.2 | async-start | bytes 2228224 | tf_op jit(solution)/shard_map/all_gather | solution.py:36
  36.0 208.2 %all-reduce.5.cloned.1.call-start = ((), (), s32[]{:S(2)}) async-start(), calls=%async_computation.7 | async-start | bytes 13631488 | tf_op jit(solution)/shard_map/psum | solution.py:49
  66.9 6.7 %copy-start.10 = (bf16[2,256,2048]{2,1,0:T(8,128)(2,1)S(1)}, bf16[2,256,2048]{2,1,0:T(8,128)(2,1)}, u32[]{:S(2)}) copy-start(bf16[2,256,2048]{2,1,0:T(8,128)(2,1)} %all-gather.4.cloned.1.call-done) | copy-start | bytes 6291460
  66.9 13.1 %slice-start = ((s8[6815744]{0:T(1024)(128)(4,1)}), s8[4194304]{0:T(1024)(128)(4,1)S(1)}, s32[]{:S(2)}) async-start(s8[6815744]{0:T(1024)(128)(4,1)} %bitcast.87), calls=%async_computation.8 | async-start | bytes 8388608
  73.6 6.4 slice-start.1
  86.6 226.7 %reduce-scatter.5.cloned.1.call-start = ((), (), s32[]{:S(2)}) async-start(), calls=%async_computation.4 | async-start | bytes 2228224 | tf_op jit(solution)/shard_map/reduce_scatter | solution.py:61
  251.7 1.5 copy-start.11
  251.7 126.0 %reduce-scatter.3.cloned.1.call-start = ((), (), s32[]{:S(2)}) async-start(), calls=%async_computation.3 | async-start | bytes 2228224 | tf_op jit(solution)/shard_map/reduce_scatter | solution.py:61
  253.1 7.1 %copy-start.5 = (bf16[2,16,2048]{2,1,0:T(8,128)(2,1)S(1)}, bf16[2,16,2048]{2,1,0:T(8,128)(2,1)}, u32[]{:S(2)}) copy-start(bf16[2,16,2048]{2,1,0:T(8,128)(2,1)} %param.13) | copy-start | bytes 393220
  260.1 119.5 %copy-start.9 = (s32[256]{0:T(256)S(1)}, s32[256]{0:T(256)}, u32[]{:S(2)}) copy-start(s32[256]{0:T(256)} %param.23) | copy-start | bytes 3076
  260.1 119.9 %copy-start.3 = (bf16[2048,3,256]{2,0,1:T(8,128)(2,1)S(1)}, bf16[2048,3,256]{2,0,1:T(8,128)(2,1)}, u32[]{:S(2)}) copy-start(bf16[2048,3,256]{2,0,1:T(8,128)(2,1)} %param.18) | copy-start | bytes 9437188
  260.2 150.0 %all-gather.8.cloned.1.call-start = ((), (), s32[]{:S(2)}) async-start(), calls=%async_computation.6 | async-start | bytes 1114112 | tf_op jit(solution)/shard_map/all_gather | solution.py:69
  379.4 64.9 %all-gather.6.cloned.1.call-start = ((), (), s32[]{:S(2)}) async-start(), calls=%async_computation.5 | async-start | bytes 1114112 | tf_op jit(solution)/shard_map/all_gather | solution.py:69
  380.0 4.6 copy-start.8
  380.0 4.8 copy-start.6
  380.1 4.8 copy-start.7
  385.5 29.4 %copy-start.4 = (bf16[2048,3,256]{0,2,1:T(8,128)(2,1)S(1)}, bf16[2048,3,256]{0,2,1:T(8,128)(2,1)}, u32[]{:S(2)}) copy-start(bf16[2048,3,256]{0,2,1:T(8,128)(2,1)} %copy.28) | copy-start | bytes 9437188
  452.2 83.3 %copy-start.1 = (bf16[32,64,256]{2,1,0:T(8,128)(2,1)S(1)}, bf16[32,64,256]{2,1,0:T(8,128)(2,1)}, u32[]{:S(2)}) copy-start(bf16[32,64,256]{2,1,0:T(8,128)(2,1)} %param.20) | copy-start | bytes 3145732
  535.6 3.3 copy-start.2
Sparse Core Ops, SparseCore 0:
  36.1 30.7 all-gather.3
  86.7 157.4 all-reduce.4
  251.8 61.4 reduce-scatter.4
  315.5 62.1 reduce-scatter.2
  379.5 30.6 all-gather.7
  411.8 32.4 all-gather.5
where the time goes:
time: 644 us
  waiting for transfers between devices  357 us (55%)
  blocking collectives  196 us (30%)
  matrix products  46.8 us (7%)
  local copies, waits for them, and re-layouts  21.8 us (3%)
  between operations  14.4 us (2%)
  other arithmetic  7.17 us (1%)
    psum x1, waiting for transfers between devices, per_device(): lax.psum((jnp.dot(normed_step, w_gate, preferred_element_type=jnp.float32...  158 us
    reduce_scatter x2, waiting for transfers between devices, per_device(): lax.psum_scatter(down_term(jnp.int32(0), local_rows * lax.axis_size('ty')...  117 us
    psum x1, blocking collectives, per_device(): lax.psum(jnp.dot(ordered, qkv_weight, preferred_element_type=jnp.float32)...  83.2 us
    psum x1, blocking collectives, per_device(): summed = lax.psum(stacked, 'ty')  52.9 us
    all_gather x2, waiting for transfers between devices, per_device(): stream_all = lax.all_gather(stream, 'ty', axis=0, tiled=True)  50.8 us
    all_gather x1, blocking collectives, per_device(): by_slot = lax.all_gather(summed, 'tx', axis=1, tiled=True)  34.4 us
    all_gather x1, waiting for transfers between devices, per_device(): normed = lax.all_gather(normed_local, 'ty', axis=1, tiled=True)  30.8 us
    psum x1, blocking collectives, per_device(): squares = lax.psum(jnp.sum(values_f * values_f, axis=2), 'tx')  25.4 us
  transfers between devices with their start and end apart: 6, of which 6 were waited for; matrix products, arithmetic and copies ran while one was open for 3% of the time, Pallas kernels for 0%

commit v1 on v0

--- a/solution.py
+++ b/solution.py
@@ -68,7 +68,10 @@
         outputs.append(stream)
         stream_all = lax.all_gather(stream, "ty", axis=0, tiled=True)
         ordered = jnp.take(stream_all, slot_rows, axis=0)
-        full = lax.psum(jnp.dot(ordered, qkv_weight, preferred_element_type=jnp.float32), "tx")
+        full = jnp.sum(
+            lax.all_gather(jnp.dot(ordered, qkv_weight, preferred_element_type=jnp.float32), "tx"),
+            axis=0,
+        )
         owned = lax.dynamic_slice_in_dim(full, lax.axis_index("tx") * owner_rows, owner_rows, 0)
         triple = owned.astype(jnp.bfloat16).reshape(owner_rows, 3, local_width)
         query = triple[:, 0]

time: 644 us -> 741 us (1.15)
  waiting for transfers between devices: 357 us -> 529 us
  blocking collectives: 196 us -> 114 us
    all_gather x0 -> x2, waiting for transfers between devices: none -> 170 us  [per_device(): lax.all_gather(jnp.dot(ordered, qkv_weight, preferred_element_type=jnp.fl...]
    psum x1 -> x0, blocking collectives: 83.2 us -> none  [per_device(): lax.psum(jnp.dot(ordered, qkv_weight, preferred_element_type=jnp.float32)...]
  transfers between devices with their start and end apart: 6 -> 8, of which waited for: 6 -> 8; matrix products, arithmetic and copies ran while one was open for 3% -> 4% of each run, Pallas kernels for 0% -> 0%
where the time goes in v1:
time: 741 us; the launch traced here: 740 us
  waiting for transfers between devices  529 us (71%)
  blocking collectives  114 us (15%)
  matrix products  46.6 us (6%)
  local copies, waits for them, and re-layouts  21.8 us (3%)
  between operations  14.4 us (2%)
  other arithmetic  13.6 us (2%)
    all_gather x2, waiting for transfers between devices, per_device(): lax.all_gather(jnp.dot(ordered, qkv_weight, preferred_element_type=jnp.fl...  170 us
    psum x1, waiting for transfers between devices, per_device(): lax.psum((jnp.dot(normed_step, w_gate, preferred_element_type=jnp.float32...  158 us
    reduce_scatter x2, waiting for transfers between devices, per_device(): lax.psum_scatter(down_term(jnp.int32(0), local_rows * lax.axis_size('ty')...  117 us
    psum x1, blocking collectives, per_device(): summed = lax.psum(stacked, 'ty')  54.6 us
    all_gather x2, waiting for transfers between devices, per_device(): stream_all = lax.all_gather(stream, 'ty', axis=0, tiled=True)  52.4 us
    all_gather x1, blocking collectives, per_device(): by_slot = lax.all_gather(summed, 'tx', axis=1, tiled=True)  34.4 us
    all_gather x1, waiting for transfers between devices, per_device(): normed = lax.all_gather(normed_local, 'ty', axis=1, tiled=True)  30.8 us
    psum x1, blocking collectives, per_device(): squares = lax.psum(jnp.sum(values_f * values_f, axis=2), 'tx')  25.4 us
  transfers between devices with their start and end apart: 8, of which 8 were waited for; matrix products, arithmetic and copies ran while one was open for 4% of the time, Pallas kernels for 0%

profile of v1, /device:TPU:0, one launch (start us, length us, event | category | flops | bytes accessed | tf_op | source)
XLA Modules:
  0.0 740.0 jit_solution(3649653066351289969)
XLA Ops:
  8.9 25.4 %psum.42 = f32[2,16]{1,0:T(2,128)S(1)} all-reduce(f32[2,16]{1,0:T(2,128)S(1)} %multiply_reduce_fusion), channel_id=1, replica_groups=mesh['tx'=8,'ty'=16] {'tx'}, use_global_device_ids=true, to_apply=%region_1.0 | all-reduce | flops 32 | bytes 256 | tf_op jit(solution)/shard_map/psum | solution.py:31
  36.0 30.8 %all-gather.8.cloned.1.call-done = bf16[2,256,2048]{2,1,0:T(8,128)(2,1)} async-done(((bf16[2,16,2048]{2,1,0:T(8,128)(2,1)}), bf16[2,256,2048]{2,1,0:T(8,128)(2,1)}) %all-gather.8.cloned.1.call-update) | async-done | bytes 2097168 | tf_op jit(solution)/shard_map/all_gather | solution.py:36
  66.9 6.7 fusion.28
  73.5 6.4 fusion.30
  79.9 3.3 fusion.29
  83.2 3.3 fusion.31
  86.5 157.6 %all-reduce.3.cloned.1.call-done = (f32[256,1664]{1,0:T(8,128)}, f32[256,1664]{1,0:T(8,128)}, f32[256,1664]{1,0:T(8,128)}, f32[256,1664]{1,0:T(8,128)}) async-done(((f32[256,1664]{1,0:T(8,128)}, f32[256,1664]{1,0:T(8,128)}, f32[256,1664]{1,0:T(8,128)}, f32[256,1664]{1,0:T(8,128)}), (f32[256,1664]{1,0:T(8,128)}, f32[256,1664]{1,0:T(8,128)}, f32[256,1664]{1,0:T(8,128)}, ...) | async-done | bytes 6815760 | tf_op jit(solution)/shard_map/psum | solution.py:49
  244.1 7.4 %fusion.33 = f32[256,2048]{1,0:T(8,128)} fusion(bf16[1664,2048]{1,0:T(8,128)(2,1)} %param.17, f32[256,1664]{1,0:T(8,128)} %get-tuple-element.11, f32[256,1664]{1,0:T(8,128)} %get-tuple-element.12), kind=kOutput, calls=%fused_computation.47 | convolution fusion | flops 1747386368 | bytes 12320768 | tf_op jit(solution)/shard_map/dot_general | solution.py:59
  253.0 7.0 fusion.32
  260.1 52.6 %reduce-scatter.5.cloned.1.call-done = f32[16,2048]{1,0:T(8,128)} async-done(((f32[256,2048]{1,0:T(8,128)}), f32[16,2048]{1,0:T(8,128)}) %reduce-scatter.5.cloned.1.call-update) | async-done | bytes 131088 | tf_op jit(solution)/shard_map/reduce_scatter | solution.py:61
  312.7 64.8 %reduce-scatter.3.cloned.1.call-done = f32[16,2048]{1,0:T(8,128)} async-done(((f32[256,2048]{1,0:T(8,128)}), f32[16,2048]{1,0:T(8,128)}) %reduce-scatter.3.cloned.1.call-update) | async-done | bytes 131088 | tf_op jit(solution)/shard_map/reduce_scatter | solution.py:61
  380.0 3.1 copy.28
  384.6 26.3 %all-gather.10.cloned.1.call-done = bf16[256,2048]{1,0:T(8,128)(2,1)} async-done(((bf16[16,2048]{1,0:T(8,128)(2,1)}), bf16[256,2048]{1,0:T(8,128)(2,1)}) %all-gather.10.cloned.1.call-update) | async-done | bytes 1048592 | tf_op jit(solution)/shard_map/all_gather | solution.py:69
  410.9 4.7 gather_fusion.1
  415.6 3.2 fusion.24
  418.9 26.1 %all-gather.12.cloned.1.call-done = bf16[256,2048]{1,0:T(8,128)(2,1)} async-done(((bf16[16,2048]{1,0:T(8,128)(2,1)}), bf16[256,2048]{1,0:T(8,128)(2,1)}) %all-gather.12.cloned.1.call-update) | async-done | bytes 1048592 | tf_op jit(solution)/shard_map/all_gather | solution.py:69
  445.0 4.7 gather_fusion.2
  449.8 3.2 fusion.22
  453.9 83.2 %all-gather.14.cloned.1.call-done = f32[2048,768]{1,0:T(8,128)} async-done(((f32[256,768]{1,0:T(8,128)}), f32[2048,768]{1,0:T(8,128)}) %all-gather.14.cloned.1.call-update) | async-done | bytes 6291472 | tf_op jit(solution)/shard_map/all_gather | solution.py:72
  537.1 3.2 reduce_sum.46
  540.3 86.6 %all-gather.16.cloned.1.call-done = f32[2048,768]{1,0:T(8,128)} async-done(((f32[256,768]{1,0:T(8,128)}), f32[2048,768]{1,0:T(8,128)}) %all-gather.16.cloned.1.call-update) | async-done | bytes 6291472 | tf_op jit(solution)/shard_map/all_gather | solution.py:72
  626.9 3.3 reduce_sum.48
  642.0 54.6 %psum.47 = f32[2,32,14]{1,2,0:T(8,128)S(1)} all-reduce(f32[2,32,14]{1,2,0:T(8,128)S(1)} %pad_maximum_fusion.5), channel_id=1, replica_groups=mesh['tx'=8,'ty'=16] {'ty'}, use_global_device_ids=true, to_apply=%region_15.17 | all-reduce | flops 896 | bytes 7168 | tf_op jit(solution)/shard_map/psum | solution.py:99
  696.7 34.4 %all_gather.31 = f32[2,256,14]{2,0,1:T(2,128)S(1)} all-gather(f32[2,32,14]{2,0,1:T(2,128)S(1)} %copy.33), channel_id=1, replica_groups=mesh['tx'=8,'ty'=16] {'tx'}, dimensions={1}, use_global_device_ids=true | all-gather | bytes 32256 | tf_op jit(solution)/shard_map/all_gather | solution.py:100
  (89 shorter events, 23.8 us)
Async XLA Ops:
  7.2 634.6 %copy-start = (bf16[256,14]{0,1:T(8,128)(2,1)S(1)}, bf16[256,14]{0,1:T(8,128)(2,1)}, u32[]{:S(2)}) copy-start(bf16[256,14]{0,1:T(8,128)(2,1)} %param.19) | copy-start | bytes 21508
  7.2 59.7 %all-gather.8.cloned.1.call-start = ((), (), s32[]{:S(2)}) async-start(), calls=%async_computation.2 | async-start | bytes 2228224 | tf_op jit(solution)/shard_map/all_gather | solution.py:36
  36.0 208.1 %all-reduce.3.cloned.1.call-start = ((), (), s32[]{:S(2)}) async-start(), calls=%async_computation.9 | async-start | bytes 13631488 | tf_op jit(solution)/shard_map/psum | solution.py:49
  66.9 6.7 copy-start.11
  73.5 6.4 copy-start.10
  86.5 226.2 %reduce-scatter.5.cloned.1.call-start = ((), (), s32[]{:S(2)}) async-start(), calls=%async_computation.4 | async-start | bytes 2228224 | tf_op jit(solution)/shard_map/reduce_scatter | solution.py:61
  251.5 1.5 copy-start.12
  251.5 125.9 %reduce-scatter.3.cloned.1.call-start = ((), (), s32[]{:S(2)}) async-start(), calls=%async_computation.3 | async-start | bytes 2228224 | tf_op jit(solution)/shard_map/reduce_scatter | solution.py:61
  253.0 7.0 copy-start.5
  259.9 120.1 %copy-start.3 = (bf16[2048,3,256]{2,0,1:T(8,128)(2,1)S(1)}, bf16[2048,3,256]{2,0,1:T(8,128)(2,1)}, u32[]{:S(2)}) copy-start(bf16[2048,3,256]{2,0,1:T(8,128)(2,1)} %param.18) | copy-start | bytes 9437188
  260.0 150.9 %all-gather.10.cloned.1.call-start = ((), (), s32[]{:S(2)}) async-start(), calls=%async_computation.5 | async-start | bytes 1114112 | tf_op jit(solution)/shard_map/all_gather | solution.py:69
  379.2 65.8 %all-gather.12.cloned.1.call-start = ((), (), s32[]{:S(2)}) async-start(), calls=%async_computation.6 | async-start | bytes 1114112 | tf_op jit(solution)/shard_map/all_gather | solution.py:69
  379.8 3.4 copy-start.9
  379.8 157.3 %all-gather.14.cloned.1.call-start = ((), (), s32[]{:S(2)}) async-start(), calls=%async_computation.7 | async-start | bytes 7077888 | tf_op jit(solution)/shard_map/all_gather | solution.py:72
  384.6 31.0 %copy-start.4 = (bf16[2048,3,256]{0,2,1:T(8,128)(2,1)S(1)}, bf16[2048,3,256]{0,2,1:T(8,128)(2,1)}, u32[]{:S(2)}) copy-start(bf16[2048,3,256]{0,2,1:T(8,128)(2,1)} %copy.28) | copy-start | bytes 9437188
  418.9 208.0 %all-gather.16.cloned.1.call-start = ((), (), s32[]{:S(2)}) async-start(), calls=%async_computation.8 | async-start | bytes 7077888 | tf_op jit(solution)/shard_map/all_gather | solution.py:72
  449.7 3.3 copy-start.8
  449.7 3.4 copy-start.6
  449.7 3.4 copy-start.7
  626.9 3.4 copy-start.1
  630.4 3.3 copy-start.2
Sparse Core Ops, SparseCore 0:
  36.1 30.7 all-gather.7
  86.6 157.4 all-reduce.2
  251.7 60.9 reduce-scatter.4
  314.9 62.5 reduce-scatter.2
  379.6 31.2 all-gather.9
  412.5 32.4 all-gather.11
  447.3 89.7 all-gather.13
  539.4 87.4 all-gather.15
